TPU v7x, 128 devices: a whole 4x4x4 slice. The times are simulated.
128 devices in a mesh: row: 8 (over x, core), col: 16 (over z, y).
Axes of the slice: x: 4, y: 4, z: 4, core: 2. Of those that a mesh axis runs over, the one named last changes fastest.
Arguments:
- ham: bfloat16 [6144, 6144], P('row', 'col'), may hold values from -0.078125 to 0.078125
- deriv: bfloat16 [6144, 6144], P('row', 'col'), may hold values from -6 to 6
- band: int32 [48], replicated, may hold values from 1 to 24, as said below
- frag_of: int32 [48], replicated, may hold values from 0 to 31
Outputs:
- sign_iterate: bfloat16 [6144, 6144], P('row', 'col')
- energy_density: bfloat16 [6144, 6144], P('row', 'col')
- pulay_terms: float32 [32, 128], P('col')
Inputs may be any that keep to these rules, and one draw needn't show every extreme that they name: Some block row has band half-width exactly 24.
All inputs are finite; a program needn't handle non-finite values.
Results may differ from a plain program's by a relative error of at most 0.006.
Values may be sent and summed in bfloat16 or wider, within the bound.
A program may use at most 64 MiB of HBM per device.

v0:
```python
import jax
import jax.numpy as jnp
from jax import lax
from jax.sharding import PartitionSpec as P

BLK = 128
FRAG_DEV = 2


def column_panel_of(right_matrix):
    return lax.all_gather(right_matrix, "row", axis=0, tiled=True)


def folded_product(left_matrix, right_matrix):
    whole_panel = column_panel_of(right_matrix)
    return jnp.dot(
        lax.all_gather(left_matrix, "col", axis=1, tiled=True),
        whole_panel,
        preferred_element_type=jnp.float32,
    )


def body(ham, deriv, band, frag_of):
    rows_here = ham.shape[0]
    cols_here = ham.shape[1]
    block_rows = rows_here // BLK
    block_cols = cols_here // BLK
    row_index = lax.axis_index("row")
    col_index = lax.axis_index("col")
    row_blocks = row_index * block_rows + jnp.arange(block_rows, dtype=jnp.int32)
    col_blocks = col_index * block_cols + jnp.arange(block_cols, dtype=jnp.int32)
    row_band = lax.dynamic_slice_in_dim(band, row_index * block_rows, block_rows)
    col_band = lax.dynamic_slice_in_dim(band, col_index * block_cols, block_cols)
    widest = jnp.maximum(row_band[:, None], col_band[None, :])
    inside = jnp.abs(row_blocks[:, None] - col_blocks[None, :]) <= widest
    pattern = jnp.repeat(jnp.repeat(inside.astype(jnp.float32), BLK, axis=0), BLK, axis=1)
    global_rows = row_index * rows_here + jnp.arange(rows_here, dtype=jnp.int32)
    global_cols = col_index * cols_here + jnp.arange(cols_here, dtype=jnp.int32)
    identity = (global_rows[:, None] == global_cols[None, :]).astype(jnp.float32)
    start = (ham.astype(jnp.float32) * pattern).astype(jnp.bfloat16)

    def start_times(right_matrix):
        return folded_product(start, right_matrix)

    square = (start_times(start) * pattern).astype(jnp.bfloat16)
    cubic = start_times(square)
    sign_iterate = (pattern * (1.5 * start.astype(jnp.float32) - 0.5 * cubic)).astype(jnp.bfloat16)
    density = (0.5 * (identity - sign_iterate.astype(jnp.float32))).astype(jnp.bfloat16)
    weighted = (start_times(density) * pattern).astype(jnp.bfloat16)
    energy_density = (folded_product(density, weighted) * pattern).astype(jnp.bfloat16)
    column_terms = jnp.sum(energy_density.astype(jnp.float32) * deriv.astype(jnp.float32), axis=0)
    column_terms = column_terms.reshape(block_cols, BLK)
    local_frags = lax.dynamic_slice_in_dim(frag_of, col_index * block_cols, block_cols)
    fragment_count = FRAG_DEV * lax.axis_size("col")
    fragments = jnp.arange(fragment_count, dtype=jnp.int32)
    onehot = (local_frags[None, :] == fragments[:, None]).astype(jnp.float32)
    partial_value = jnp.dot(onehot, column_terms, precision=lax.Precision.HIGHEST)
    grand_total = lax.psum(partial_value, ("row", "col"))
    pulay_terms = lax.dynamic_slice_in_dim(grand_total, col_index * FRAG_DEV, FRAG_DEV, 0)
    return (sign_iterate, energy_density, pulay_terms)


def solution(mesh):
    placed = (P("row", "col"), P("row", "col"), P(), P())
    return jax.shard_map(
        body,
        mesh=mesh,
        in_specs=placed,
        out_specs=(P("row", "col"), P("row", "col"), P("col", None)),
        check_vma=False,
    )
```

profile of v0, /device:TPU:1, one launch (start us, length us, event | category | flops | bytes accessed | tf_op | source)
XLA Modules:
  0.0 432.5 jit_solution(7368020755092818838)
XLA Ops:
  7.2 0.7 dynamic_slice.13
  8.0 0.7 dynamic_slice.12
  8.7 0.1 fusion.9
  8.9 0.1 broadcast_in_dim.5
  9.0 0.4 copy.8
  9.3 0.7 copy-done
  10.0 0.9 multiply_convert_fusion.1
  11.0 0.7 all-gather.7.cloned.1.call-update
  11.8 37.2 %all-gather.9.cloned.1.call-done = bf16[6144,384]{1,0:T(8,128)(2,1)} async-done(((bf16[768,384]{1,0:T(8,128)(2,1)}), bf16[6144,384]{1,0:T(8,128)(2,1)}) %all-gather.9.cloned.1.call-update) | async-done | bytes 4718608 | tf_op jit(solution)/shard_map/all_gather | solution.py:11
  48.9 83.6 %all-gather.7.cloned.1.call-done = bf16[768,6144]{1,0:T(8,128)(2,1)} async-done(((bf16[768,384]{1,0:T(8,128)(2,1)}), bf16[768,6144]{1,0:T(8,128)(2,1)}) %all-gather.7.cloned.1.call-update) | async-done | bytes 9437200 | tf_op jit(solution)/shard_map/all_gather | solution.py:17
  132.5 9.7 %fusion.3 = bf16[768,384]{0,1:T(8,128)(2,1)} fusion(f32[768,384]{0,1:T(8,128)S(1)} %bitcast.20, bf16[768,6144]{1,0:T(8,128)(2,1)} %all-gather.7.cloned.1.call-done, bf16[6144,384]{1,0:T(8,128)(2,1)} %all-gather.9.cloned.1.call-done), kind=kOutput, calls=%fused_computation.7 | convolution fusion | flops 3624468480 | bytes 15925248 | tf_op jit(solution)/shard_map/dot_general | solution.py:16
  142.3 35.3 %all-gather.11.cloned.1.call-done = bf16[6144,384]{0,1:T(8,128)(2,1)} async-done(((bf16[768,384]{0,1:T(8,128)(2,1)}), bf16[6144,384]{0,1:T(8,128)(2,1)}) %all-gather.11.cloned.1.call-update) | async-done | bytes 4718608 | tf_op jit(solution)/shard_map/all_gather | solution.py:11
  177.6 10.0 %multiply_convert_fusion = (bf16[768,384]{1,0:T(8,128)(2,1)}, bf16[768,384]{1,0:T(8,128)(2,1)}) fusion(s32[384]{0:T(512)S(1)} %iota_add_fusion.1, s32[768]{0:T(1024)S(1)} %iota_add_fusion, f32[768,384]{1,0:T(8,128)S(1)} %copy.8, bf16[768,6144]{1,0:T(8,128)(2,1)} %all-gather.7.cloned.1.call-done, bf16[6144,384]{0,1:T(8,128)(2,1)} %all-gather.11.cloned.1.call-done, ...), kind=kOutput, calls=%fused_computation.11 | convolution fusion | flops 3628302336 | bytes 17109504 | tf_op jit(solution)/shard_map/dot_general | solution.py:16
  187.7 34.3 %all-gather.15.cloned.1.call-done = bf16[6144,384]{1,0:T(8,128)(2,1)} async-done(((bf16[768,384]{1,0:T(8,128)(2,1)}), bf16[6144,384]{1,0:T(8,128)(2,1)}) %all-gather.15.cloned.1.call-update) | async-done | bytes 4718608 | tf_op jit(solution)/shard_map/all_gather | solution.py:11
  222.0 9.7 %fusion.4 = bf16[768,384]{0,1:T(8,128)(2,1)} fusion(f32[768,384]{0,1:T(8,128)S(1)} %bitcast.21, bf16[768,6144]{1,0:T(8,128)(2,1)} %all-gather.7.cloned.1.call-done, bf16[6144,384]{1,0:T(8,128)(2,1)} %all-gather.15.cloned.1.call-done), kind=kOutput, calls=%fused_computation.8 | convolution fusion | flops 3624468480 | bytes 15925248 | tf_op jit(solution)/shard_map/dot_general | solution.py:16
  231.7 0.2 all-gather.13.cloned.1.call-start
  231.9 0.3 all-gather.13.cloned.1.call-update
  232.3 0.1 dynamic_slice.14
  232.4 33.7 %all-gather.17.cloned.1.call-done = bf16[6144,384]{0,1:T(8,128)(2,1)} async-done(((bf16[768,384]{0,1:T(8,128)(2,1)}), bf16[6144,384]{0,1:T(8,128)(2,1)}) %all-gather.17.cloned.1.call-update) | async-done | bytes 4718608 | tf_op jit(solution)/shard_map/all_gather | solution.py:11
  266.1 83.4 %all-gather.13.cloned.1.call-done = bf16[768,6144]{1,0:T(8,128)(2,1)} async-done(((bf16[768,384]{1,0:T(8,128)(2,1)}), bf16[768,6144]{1,0:T(8,128)(2,1)}) %all-gather.13.cloned.1.call-update) | async-done | bytes 9437200 | tf_op jit(solution)/shard_map/all_gather | solution.py:17
  349.5 9.8 %multiply_reduce_fusion = (f32[384]{0:T(512)S(1)}, bf16[768,384]{1,0:T(8,128)(2,1)}) fusion(bf16[768,384]{1,0:T(8,128)(2,1)S(1)} %copy-done.1, f32[768,384]{1,0:T(8,128)S(1)} %copy.8, bf16[768,6144]{1,0:T(8,128)(2,1)} %all-gather.13.cloned.1.call-done, bf16[6144,384]{0,1:T(8,128)(2,1)} %all-gather.17.cloned.1.call-done), kind=kOutput, calls=%fused_computation.10 | convolution fusion | flops 3625647616 | bytes 16516608 | tf_op jit(solution)/shard_map/dot_general | solution.py:16
  359.3 0.1 fusion.6
  359.4 65.7 %psum.7 = f32[32,128]{1,0:T(8,128)S(1)} all-reduce(f32[32,128]{1,0:T(8,128)S(1)} %fusion.6), channel_id=1, replica_groups=mesh['row'=8,'col'=16] {'row','col'}, use_global_device_ids=true, to_apply=%region_1.0 | all-reduce | flops 4096 | bytes 32768 | tf_op jit(solution)/shard_map/psum | solution.py:58
  425.1 0.6 constant_dynamic-slice_fusion
  (20 shorter events, 0.4 us)
Async XLA Ops:
  7.2 41.8 %all-gather.9.cloned.1.call-start = ((), (), s32[]{:S(2)}) async-start(), calls=%async_computation.1 | async-start | bytes 5308416 | tf_op jit(solution)/shard_map/all_gather | solution.py:11
  9.0 1.1 copy-start
  11.0 121.6 %all-gather.7.cloned.1.call-start = ((), (), s32[]{:S(2)}) async-start(), calls=%async_computation | async-start | bytes 10027008 | tf_op jit(solution)/shard_map/all_gather | solution.py:17
  11.7 165.9 %all-gather.11.cloned.1.call-start = ((), (), s32[]{:S(2)}) async-start(), calls=%async_computation.2 | async-start | bytes 5308416 | tf_op jit(solution)/shard_map/all_gather | solution.py:11
  142.3 79.7 %all-gather.15.cloned.1.call-start = ((), (), s32[]{:S(2)}) async-start(), calls=%async_computation.4 | async-start | bytes 5308416 | tf_op jit(solution)/shard_map/all_gather | solution.py:11
  187.6 78.5 %all-gather.17.cloned.1.call-start = ((), (), s32[]{:S(2)}) async-start(), calls=%async_computation.5 | async-start | bytes 5308416 | tf_op jit(solution)/shard_map/all_gather | solution.py:11
  231.7 0.7 copy-start.2
  231.7 117.8 %copy-start.1 = (bf16[768,384]{1,0:T(8,128)(2,1)S(1)}, bf16[768,384]{1,0:T(8,128)(2,1)}, u32[]{:S(2)}) copy-start(bf16[768,384]{1,0:T(8,128)(2,1)} %param.5) | copy-start | bytes 1769476
  231.7 117.8 %all-gather.13.cloned.1.call-start = ((), (), s32[]{:S(2)}) async-start(), calls=%async_computation.3 | async-start | bytes 10027008 | tf_op jit(solution)/shard_map/all_gather | solution.py:17
Sparse Core Ops, SparseCore 0:
  11.1 37.7 all-gather.8
  51.6 80.8 all-gather.6
  142.4 35.1 all-gather.10
  187.7 34.2 all-gather.14
  231.8 34.2 all-gather.16
  268.6 80.8 all-gather.12
where the time goes:
time: 433 us
  waiting for transfers between devices  309 us (71%)
  blocking collectives  65.7 us (15%)
  matrix products  39.3 us (9%)
  between operations  14.2 us (3%)
    all_gather x2, waiting for transfers between devices, folded_product(): lax.all_gather(left_matrix, 'col', axis=1, tiled=True)  167 us
    all_gather x4, waiting for transfers between devices, column_panel_of(): return lax.all_gather(right_matrix, 'row', axis=0, tiled=True)  140 us
    psum x1, blocking collectives, body(): grand_total = lax.psum(partial_value, ('row', 'col'))  65.7 us
    dot_general x4, matrix products, folded_product(): jnp.dot(lax.all_gather(left_matrix, 'col', axis=1, tiled=True), whole_pan...  39.1 us
  transfers between devices with their start and end apart: 6, of which 6 were waited for; matrix products, arithmetic and copies ran while one was open for 0% of the time, Pallas kernels for 0%

commit v1 on v0

--- a/solution.py
+++ b/solution.py
@@ -7,6 +7,27 @@
 FRAG_DEV = 2
 
 
+def ring_gather(value, axis, dim):
+    size, place, extent = (lax.axis_size(axis), lax.axis_index(axis), value.shape[dim])
+    right = [(i, (i + 1) % size) for i in range(size)]
+    left = [(i, (i - 1) % size) for i in range(size)]
+    result = jnp.zeros((*value.shape[:dim], size * extent, *value.shape[dim + 1 :]), value.dtype)
+    result = lax.dynamic_update_slice_in_dim(result, value, place * extent, axis=dim)
+    from_left = from_right = value
+    half = size // 2
+    for step in range(1, half + 1):
+        from_left = lax.ppermute(from_left, axis, right)
+        result = lax.dynamic_update_slice_in_dim(
+            result, from_left, (place - step) % size * extent, axis=dim
+        )
+        if step < size - half:
+            from_right = lax.ppermute(from_right, axis, left)
+            result = lax.dynamic_update_slice_in_dim(
+                result, from_right, (place + step) % size * extent, axis=dim
+            )
+    return result
+
+
 def column_panel_of(right_matrix):
     return lax.all_gather(right_matrix, "row", axis=0, tiled=True)
 
@@ -14,9 +35,7 @@
 def folded_product(left_matrix, right_matrix):
     whole_panel = column_panel_of(right_matrix)
     return jnp.dot(
-        lax.all_gather(left_matrix, "col", axis=1, tiled=True),
-        whole_panel,
-        preferred_element_type=jnp.float32,
+        ring_gather(left_matrix, "col", 1), whole_panel, preferred_element_type=jnp.float32
     )
 
 

time: 433 us -> 453 us (1.046)
  waiting for transfers between devices: 309 us -> 202 us
  starting transfers between devices: 0.42 us -> 70.4 us
  local copies, waits for them, and re-layouts: 3.37 us -> 57.8 us
    all_gather x2 -> x0, waiting for transfers between devices: 167 us -> none  [folded_product(): lax.all_gather(left_matrix, 'col', axis=1, tiled=True)]
    ppermute x0 -> x30, waiting for transfers between devices: none -> 130 us  [the longest x16 130 us: ring_gather(): from_left = lax.ppermute(from_left, axis, right)]
    ppermute x0 -> x30, starting transfers between devices: none -> 70.2 us  [the longest x14 66.6 us: ring_gather(): from_right = lax.ppermute(from_right, axis, left)]
    all_gather x4, waiting for transfers between devices: 140 us -> 71.8 us  [column_panel_of(): return lax.all_gather(right_matrix, 'row', axis=0, tiled=True)]
    dynamic_update_slice x0 -> x30, local copies, waits for them, and re-layouts: none -> 45.4 us  [the longest x16 23.7 us: ring_gather(): lax.dynamic_update_slice_in_dim(result, from_left, (place - step) % size...]
    another operation x0 -> x2, local copies, waits for them, and re-layouts: none -> 9.64 us
  transfers between devices with their start and end apart: 6 -> 34, of which waited for: 6 -> 17; matrix products, arithmetic and copies ran while one was open for 0% -> 10% of each run, Pallas kernels for 0% -> 0%
where the time goes in v1:
time: 453 us; the launch traced here: 452 us
  waiting for transfers between devices  202 us (45%)
  starting transfers between devices  70.4 us (16%)
  blocking collectives  69.1 us (15%)
  local copies, waits for them, and re-layouts  57.8 us (13%)
  matrix products  38 us (8%)
  between operations  14 us (3%)
    ppermute x16, waiting for transfers between devices, ring_gather(): from_left = lax.ppermute(from_left, axis, right)  130 us
    all_gather x4, waiting for transfers between devices, column_panel_of(): return lax.all_gather(right_matrix, 'row', axis=0, tiled=True)  71.8 us
    psum x1, blocking collectives, body(): grand_total = lax.psum(partial_value, ('row', 'col'))  69.1 us
    ppermute x14, starting transfers between devices, ring_gather(): from_right = lax.ppermute(from_right, axis, left)  66.6 us
    dot_general x4, matrix products, folded_product(): jnp.dot(ring_gather(left_matrix, 'col', 1), whole_panel, preferred_elemen...  37.9 us
    dynamic_update_slice x16, local copies, waits for them, and re-layouts, ring_gather(): lax.dynamic_update_slice_in_dim(result, from_left, (place - step) % size...  23.7 us
    dynamic_update_slice x14, local copies, waits for them, and re-layouts, ring_gather(): lax.dynamic_update_slice_in_dim(result, from_right, (place + step) % size...  21.7 us
    another operation x2, local copies, waits for them, and re-layouts  9.64 us
  transfers between devices with their start and end apart: 34, of which 17 were waited for; matrix products, arithmetic and copies ran while one was open for 10% of the time, Pallas kernels for 0%

profile of v1, /device:TPU:1, one launch (start us, length us, event | category | flops | bytes accessed | tf_op | source)
XLA Modules:
  0.0 452.1 jit_solution(13396589840212585847)
XLA Ops:
  17.8 4.9 %collective-permute-start.1 = (bf16[768,384]{1,0:T(8,128)(2,1)}, bf16[768,384]{1,0:T(8,128)(2,1)S(1)}, u32[]{:S(2)}, u32[]{:S(2)}) collective-permute-start(bf16[768,384]{1,0:T(8,128)(2,1)} %get-tuple-element.6), channel_id=1, source_target_pairs={{0,15},{1,0},{2,1},{3,2},{4,3},{5,4},{6,5},{7,6},{8,7},{9,8},{10,9... | collective-permute-start | bytes 1769480 | tf_op jit(solution)/shard_map/ppermute | solution.py:24
  22.7 13.2 %collective-permute-done = bf16[768,384]{1,0:T(8,128)(2,1)S(1)} collective-permute-done((bf16[768,384]{1,0:T(8,128)(2,1)}, bf16[768,384]{1,0:T(8,128)(2,1)S(1)}, u32[]{:S(2)}, u32[]{:S(2)}) %collective-permute-start) | collective-permute-done | bytes 589856 | tf_op jit(solution)/shard_map/ppermute | solution.py:19
  40.6 12.2 %collective-permute-done.2 = bf16[768,384]{1,0:T(8,128)(2,1)S(1)} collective-permute-done((bf16[768,384]{1,0:T(8,128)(2,1)S(1)}, bf16[768,384]{1,0:T(8,128)(2,1)S(1)}, u32[]{:S(2)}, u32[]{:S(2)}) %collective-permute-start.2) | collective-permute-done | bytes 589856 | tf_op jit(solution)/shard_map/ppermute | solution.py:19
  57.6 11.3 %collective-permute-done.4 = bf16[768,384]{1,0:T(8,128)(2,1)S(1)} collective-permute-done((bf16[768,384]{1,0:T(8,128)(2,1)S(1)}, bf16[768,384]{1,0:T(8,128)(2,1)S(1)}, u32[]{:S(2)}, u32[]{:S(2)}) %collective-permute-start.4) | collective-permute-done | bytes 589856 | tf_op jit(solution)/shard_map/ppermute | solution.py:19
  73.7 10.5 %collective-permute-done.6 = bf16[768,384]{1,0:T(8,128)(2,1)S(1)} collective-permute-done((bf16[768,384]{1,0:T(8,128)(2,1)S(1)}, bf16[768,384]{1,0:T(8,128)(2,1)S(1)}, u32[]{:S(2)}, u32[]{:S(2)}) %collective-permute-start.6) | collective-permute-done | bytes 589856 | tf_op jit(solution)/shard_map/ppermute | solution.py:19
  89.0 9.6 %collective-permute-done.8 = bf16[768,384]{1,0:T(8,128)(2,1)} collective-permute-done((bf16[768,384]{1,0:T(8,128)(2,1)S(1)}, bf16[768,384]{1,0:T(8,128)(2,1)}, u32[]{:S(2)}, u32[]{:S(2)}) %collective-permute-start.8) | collective-permute-done | bytes 589856 | tf_op jit(solution)/shard_map/ppermute | solution.py:19
  133.1 5.2 %collective-permute-done.14 = bf16[768,384]{1,0:T(8,128)(2,1)S(1)} collective-permute-done((bf16[768,384]{1,0:T(8,128)(2,1)S(1)}, bf16[768,384]{1,0:T(8,128)(2,1)S(1)}, u32[]{:S(2)}, u32[]{:S(2)}) %collective-permute-start.14) | collective-permute-done | bytes 589856 | tf_op jit(solution)/shard_map/ppermute | solution.py:19
  139.2 9.7 %fusion.3 = bf16[768,384]{0,1:T(8,128)(2,1)} fusion(f32[768,384]{0,1:T(8,128)S(1)} %bitcast.20, bf16[768,6144]{1,0:T(8,128)(2,1)} %constant_dynamic-update-slice_fusion.16, bf16[6144,384]{1,0:T(8,128)(2,1)} %all-gather.5.cloned.1.call-done), kind=kOutput, calls=%fused_computation.7 | convolution fusion | flops 3624468480 | bytes 15925248 | tf_op jit(solution)/shard_map/dot_general | solution.py:37
  149.0 37.5 %all-gather.7.cloned.1.call-done = bf16[6144,384]{0,1:T(8,128)(2,1)} async-done(((bf16[768,384]{0,1:T(8,128)(2,1)}), bf16[6144,384]{0,1:T(8,128)(2,1)}) %all-gather.7.cloned.1.call-update) | async-done | bytes 4718608 | tf_op jit(solution)/shard_map/all_gather | solution.py:32
  191.3 8.6 %constant_dynamic-update-slice_fusion.15 = (bf16[768,6144]{1,0:T(8,128)(2,1)}, bf16[768,384]{1,0:T(8,128)(2,1)}, bf16[768,384]{1,0:T(8,128)(2,1)}) fusion(bf16[768,6144]{1,0:T(8,128)(2,1)} %broadcast.40, s32[]{:T(128)S(6)} %select_n.261, s32[384]{0:T(512)S(1)} %iota_add_fusion.1, s32[768]{0:T(1024)S(1)} %iota_add_fusion, f32[768,384]{1,0:T(8,128)S(1)} %copy.8, ...), kind=kOutput, calls=%fused_computation.32 | convolution fusion | flops 3627417600 | bytes 17699332 | tf_op jit(solution)/shard_map/dot_general | solution.py:37
  200.1 34.3 %all-gather.9.cloned.1.call-done = bf16[6144,384]{1,0:T(8,128)(2,1)} async-done(((bf16[768,384]{1,0:T(8,128)(2,1)}), bf16[6144,384]{1,0:T(8,128)(2,1)}) %all-gather.9.cloned.1.call-update) | async-done | bytes 4718608 | tf_op jit(solution)/shard_map/all_gather | solution.py:32
  234.4 9.7 %fusion.4 = bf16[768,384]{0,1:T(8,128)(2,1)} fusion(f32[768,384]{0,1:T(8,128)S(1)} %bitcast.21, bf16[768,6144]{1,0:T(8,128)(2,1)} %constant_dynamic-update-slice_fusion.16, bf16[6144,384]{1,0:T(8,128)(2,1)} %all-gather.9.cloned.1.call-done), kind=kOutput, calls=%fused_computation.8 | convolution fusion | flops 3624468480 | bytes 15925248 | tf_op jit(solution)/shard_map/dot_general | solution.py:37
  249.3 12.9 %collective-permute-done.15 = bf16[768,384]{1,0:T(8,128)(2,1)S(1)} collective-permute-done((bf16[768,384]{1,0:T(8,128)(2,1)S(1)}, bf16[768,384]{1,0:T(8,128)(2,1)S(1)}, u32[]{:S(2)}, u32[]{:S(2)}) %collective-permute-start.15) | collective-permute-done | bytes 589856 | tf_op jit(solution)/shard_map/ppermute | solution.py:19
  262.2 5.0 %collective-permute-start.18 = (bf16[768,384]{1,0:T(8,128)(2,1)S(1)}, bf16[768,384]{1,0:T(8,128)(2,1)S(1)}, u32[]{:S(2)}, u32[]{:S(2)}) collective-permute-start(bf16[768,384]{1,0:T(8,128)(2,1)S(1)} %collective-permute-done.16), channel_id=1, source_target_pairs={{0,15},{1,0},{2,1},{3,2},{4,3},{5,4},{6,5},{7,6},{8,7},{9,8},{10,9... | collective-permute-start | bytes 1769480 | tf_op jit(solution)/shard_map/ppermute | solution.py:24
  267.2 12.1 %collective-permute-done.17 = bf16[768,384]{1,0:T(8,128)(2,1)S(1)} collective-permute-done((bf16[768,384]{1,0:T(8,128)(2,1)S(1)}, bf16[768,384]{1,0:T(8,128)(2,1)S(1)}, u32[]{:S(2)}, u32[]{:S(2)}) %collective-permute-start.17) | collective-permute-done | bytes 589856 | tf_op jit(solution)/shard_map/ppermute | solution.py:19
  279.4 4.9 %collective-permute-start.20 = (bf16[768,384]{1,0:T(8,128)(2,1)S(1)}, bf16[768,384]{1,0:T(8,128)(2,1)S(1)}, u32[]{:S(2)}, u32[]{:S(2)}) collective-permute-start(bf16[768,384]{1,0:T(8,128)(2,1)S(1)} %collective-permute-done.18), channel_id=1, source_target_pairs={{0,15},{1,0},{2,1},{3,2},{4,3},{5,4},{6,5},{7,6},{8,7},{9,8},{10,9... | collective-permute-start | bytes 1769480 | tf_op jit(solution)/shard_map/ppermute | solution.py:24
  284.3 11.3 %collective-permute-done.19 = bf16[768,384]{1,0:T(8,128)(2,1)S(1)} collective-permute-done((bf16[768,384]{1,0:T(8,128)(2,1)S(1)}, bf16[768,384]{1,0:T(8,128)(2,1)S(1)}, u32[]{:S(2)}, u32[]{:S(2)}) %collective-permute-start.19) | collective-permute-done | bytes 589856 | tf_op jit(solution)/shard_map/ppermute | solution.py:19
  295.7 4.8 %collective-permute-start.22 = (bf16[768,384]{1,0:T(8,128)(2,1)S(1)}, bf16[768,384]{1,0:T(8,128)(2,1)}, u32[]{:S(2)}, u32[]{:S(2)}) collective-permute-start(bf16[768,384]{1,0:T(8,128)(2,1)S(1)} %collective-permute-done.20), channel_id=1, source_target_pairs={{0,15},{1,0},{2,1},{3,2},{4,3},{5,4},{6,5},{7,6},{8,7},{9,8},{10,9... | collective-permute-start | bytes 1769480 | tf_op jit(solution)/shard_map/ppermute | solution.py:24
  300.5 10.6 %collective-permute-done.21 = bf16[768,384]{1,0:T(8,128)(2,1)S(1)} collective-permute-done((bf16[768,384]{1,0:T(8,128)(2,1)S(1)}, bf16[768,384]{1,0:T(8,128)(2,1)S(1)}, u32[]{:S(2)}, u32[]{:S(2)}) %collective-permute-start.21) | collective-permute-done | bytes 589856 | tf_op jit(solution)/shard_map/ppermute | solution.py:19
  311.1 4.8 %collective-permute-start.24 = (bf16[768,384]{1,0:T(8,128)(2,1)}, bf16[768,384]{1,0:T(8,128)(2,1)S(1)}, u32[]{:S(2)}, u32[]{:S(2)}) collective-permute-start(bf16[768,384]{1,0:T(8,128)(2,1)} %collective-permute-done.22), channel_id=1, source_target_pairs={{0,15},{1,0},{2,1},{3,2},{4,3},{5,4},{6,5},{7,6},{8,7},{9,8},{10,9... | collective-permute-start | bytes 1769480 | tf_op jit(solution)/shard_map/ppermute | solution.py:24
  315.9 9.8 %collective-permute-done.23 = bf16[768,384]{1,0:T(8,128)(2,1)} collective-permute-done((bf16[768,384]{1,0:T(8,128)(2,1)S(1)}, bf16[768,384]{1,0:T(8,128)(2,1)}, u32[]{:S(2)}, u32[]{:S(2)}) %collective-permute-start.23) | collective-permute-done | bytes 589856 | tf_op jit(solution)/shard_map/ppermute | solution.py:19
  358.6 6.3 %collective-permute-done.29 = bf16[768,384]{1,0:T(8,128)(2,1)S(1)} collective-permute-done((bf16[768,384]{1,0:T(8,128)(2,1)S(1)}, bf16[768,384]{1,0:T(8,128)(2,1)S(1)}, u32[]{:S(2)}, u32[]{:S(2)}) %collective-permute-start.29) | collective-permute-done | bytes 589856 | tf_op jit(solution)/shard_map/ppermute | solution.py:19
  365.9 9.9 %multiply_reduce_fusion = (f32[384]{0:T(512)S(1)}, bf16[768,384]{1,0:T(8,128)(2,1)}) fusion(bf16[768,384]{1,0:T(8,128)(2,1)} %param.5, f32[768,384]{1,0:T(8,128)S(1)} %copy.8, bf16[768,6144]{1,0:T(8,128)(2,1)} %constant_dynamic-update-slice_fusion, bf16[6144,384]{0,1:T(8,128)(2,1)} %all-gather.11.cloned.1.call-done), kind=kOutput, calls=%fused_computation.10 | convolution fusion | flops 3625647616 | bytes 16516608 | tf_op jit(solution)/shard_map/dot_general | solution.py:37
  375.9 69.1 %psum.7 = f32[32,128]{1,0:T(8,128)S(1)} all-reduce(f32[32,128]{1,0:T(8,128)S(1)} %fusion.6), channel_id=1, replica_groups=mesh['row'=8,'col'=16] {'row','col'}, use_global_device_ids=true, to_apply=%region_1.2 | all-reduce | flops 4096 | bytes 32768 | tf_op jit(solution)/shard_map/psum | solution.py:77
  (128 shorter events, 109.8 us)
Async XLA Ops:
  7.2 132.0 %all-gather.5.cloned.1.call-start = ((), (), s32[]{:S(2)}) async-start(), calls=%async_computation | async-start | bytes 5308416 | tf_op jit(solution)/shard_map/all_gather | solution.py:32
  15.5 171.0 %all-gather.7.cloned.1.call-start = ((), (), s32[]{:S(2)}) async-start(), calls=%async_computation.1 | async-start | bytes 5308416 | tf_op jit(solution)/shard_map/all_gather | solution.py:32
  15.5 20.3 %collective-permute-start = (bf16[768,384]{1,0:T(8,128)(2,1)}, bf16[768,384]{1,0:T(8,128)(2,1)S(1)}, u32[]{:S(2)}, u32[]{:S(2)}) collective-permute-start(bf16[768,384]{1,0:T(8,128)(2,1)} %get-tuple-element.6), channel_id=1, source_target_pairs={{0,1},{1,2},{2,3},{3,4},{4,5},{5,6},{6,7},{7,8},{8,9},{9,10},{10,1... | collective-permute-start | bytes 1769480 | tf_op jit(solution)/shard_map/ppermute | solution.py:19
  17.8 18.1 %collective-permute-start.1 = (bf16[768,384]{1,0:T(8,128)(2,1)}, bf16[768,384]{1,0:T(8,128)(2,1)S(1)}, u32[]{:S(2)}, u32[]{:S(2)}) collective-permute-start(bf16[768,384]{1,0:T(8,128)(2,1)} %get-tuple-element.6), channel_id=1, source_target_pairs={{0,15},{1,0},{2,1},{3,2},{4,3},{5,4},{6,5},{7,6},{8,7},{9,8},{10,9... | collective-permute-start | bytes 1769480 | tf_op jit(solution)/shard_map/ppermute | solution.py:24
  35.8 17.0 %collective-permute-start.2 = (bf16[768,384]{1,0:T(8,128)(2,1)S(1)}, bf16[768,384]{1,0:T(8,128)(2,1)S(1)}, u32[]{:S(2)}, u32[]{:S(2)}) collective-permute-start(bf16[768,384]{1,0:T(8,128)(2,1)S(1)} %collective-permute-done), channel_id=1, source_target_pairs={{0,1},{1,2},{2,3},{3,4},{4,5},{5,6},{6,7},{7,8},{8,9},{9,10},{10,1... | collective-permute-start | bytes 1769480 | tf_op jit(solution)/shard_map/ppermute | solution.py:19
  35.9 17.0 %collective-permute-start.3 = (bf16[768,384]{1,0:T(8,128)(2,1)S(1)}, bf16[768,384]{1,0:T(8,128)(2,1)S(1)}, u32[]{:S(2)}, u32[]{:S(2)}) collective-permute-start(bf16[768,384]{1,0:T(8,128)(2,1)S(1)} %collective-permute-done.1), channel_id=1, source_target_pairs={{0,15},{1,0},{2,1},{3,2},{4,3},{5,4},{6,5},{7,6},{8,7},{9,8},{10,9... | collective-permute-start | bytes 1769480 | tf_op jit(solution)/shard_map/ppermute | solution.py:24
  52.8 16.1 %collective-permute-start.4 = (bf16[768,384]{1,0:T(8,128)(2,1)S(1)}, bf16[768,384]{1,0:T(8,128)(2,1)S(1)}, u32[]{:S(2)}, u32[]{:S(2)}) collective-permute-start(bf16[768,384]{1,0:T(8,128)(2,1)S(1)} %collective-permute-done.2), channel_id=1, source_target_pairs={{0,1},{1,2},{2,3},{3,4},{4,5},{5,6},{6,7},{7,8},{8,9},{9,10},{10,1... | collective-permute-start | bytes 1769480 | tf_op jit(solution)/shard_map/ppermute | solution.py:19
  52.8 16.1 %collective-permute-start.5 = (bf16[768,384]{1,0:T(8,128)(2,1)S(1)}, bf16[768,384]{1,0:T(8,128)(2,1)S(1)}, u32[]{:S(2)}, u32[]{:S(2)}) collective-permute-start(bf16[768,384]{1,0:T(8,128)(2,1)S(1)} %collective-permute-done.3), channel_id=1, source_target_pairs={{0,15},{1,0},{2,1},{3,2},{4,3},{5,4},{6,5},{7,6},{8,7},{9,8},{10,9... | collective-permute-start | bytes 1769480 | tf_op jit(solution)/shard_map/ppermute | solution.py:24
  68.9 15.2 %collective-permute-start.6 = (bf16[768,384]{1,0:T(8,128)(2,1)S(1)}, bf16[768,384]{1,0:T(8,128)(2,1)S(1)}, u32[]{:S(2)}, u32[]{:S(2)}) collective-permute-start(bf16[768,384]{1,0:T(8,128)(2,1)S(1)} %collective-permute-done.4), channel_id=1, source_target_pairs={{0,1},{1,2},{2,3},{3,4},{4,5},{5,6},{6,7},{7,8},{8,9},{9,10},{10,1... | collective-permute-start | bytes 1769480 | tf_op jit(solution)/shard_map/ppermute | solution.py:19
  68.9 15.3 %collective-permute-start.7 = (bf16[768,384]{1,0:T(8,128)(2,1)S(1)}, bf16[768,384]{1,0:T(8,128)(2,1)}, u32[]{:S(2)}, u32[]{:S(2)}) collective-permute-start(bf16[768,384]{1,0:T(8,128)(2,1)S(1)} %collective-permute-done.5), channel_id=1, source_target_pairs={{0,15},{1,0},{2,1},{3,2},{4,3},{5,4},{6,5},{7,6},{8,7},{9,8},{10,9... | collective-permute-start | bytes 1769480 | tf_op jit(solution)/shard_map/ppermute | solution.py:24
  84.2 19.5 %collective-permute-start.9 = (bf16[768,384]{1,0:T(8,128)(2,1)}, bf16[768,384]{1,0:T(8,128)(2,1)}, u32[]{:S(2)}, u32[]{:S(2)}) collective-permute-start(bf16[768,384]{1,0:T(8,128)(2,1)} %collective-permute-done.7), channel_id=1, source_target_pairs={{0,15},{1,0},{2,1},{3,2},{4,3},{5,4},{6,5},{7,6},{8,7},{9,8},{10,9... | collective-permute-start | bytes 1769480 | tf_op jit(solution)/shard_map/ppermute | solution.py:24
  103.7 15.8 %collective-permute-start.11 = (bf16[768,384]{1,0:T(8,128)(2,1)}, bf16[768,384]{1,0:T(8,128)(2,1)S(1)}, u32[]{:S(2)}, u32[]{:S(2)}) collective-permute-start(bf16[768,384]{1,0:T(8,128)(2,1)} %collective-permute-done.9), channel_id=1, source_target_pairs={{0,15},{1,0},{2,1},{3,2},{4,3},{5,4},{6,5},{7,6},{8,7},{9,8},{10,9... | collective-permute-start | bytes 1769480 | tf_op jit(solution)/shard_map/ppermute | solution.py:24
  148.9 85.5 %all-gather.9.cloned.1.call-start = ((), (), s32[]{:S(2)}) async-start(), calls=%async_computation.2 | async-start | bytes 5308416 | tf_op jit(solution)/shard_map/all_gather | solution.py:32
  200.0 165.9 %all-gather.11.cloned.1.call-start = ((), (), s32[]{:S(2)}) async-start(), calls=%async_computation.3 | async-start | bytes 5308416 | tf_op jit(solution)/shard_map/all_gather | solution.py:32
  244.1 18.1 %collective-permute-start.15 = (bf16[768,384]{1,0:T(8,128)(2,1)S(1)}, bf16[768,384]{1,0:T(8,128)(2,1)S(1)}, u32[]{:S(2)}, u32[]{:S(2)}) collective-permute-start(bf16[768,384]{1,0:T(8,128)(2,1)S(1)} %copy-done.10), channel_id=1, source_target_pairs={{0,1},{1,2},{2,3},{3,4},{4,5},{5,6},{6,7},{7,8},{8,9},{9,10},{10,1... | collective-permute-start | bytes 1769480 | tf_op jit(solution)/shard_map/ppermute | solution.py:19
  245.4 16.9 %collective-permute-start.16 = (bf16[768,384]{1,0:T(8,128)(2,1)S(1)}, bf16[768,384]{1,0:T(8,128)(2,1)S(1)}, u32[]{:S(2)}, u32[]{:S(2)}) collective-permute-start(bf16[768,384]{1,0:T(8,128)(2,1)S(1)} %copy-done.10), channel_id=1, source_target_pairs={{0,15},{1,0},{2,1},{3,2},{4,3},{5,4},{6,5},{7,6},{8,7},{9,8},{10,9... | collective-permute-start | bytes 1769480 | tf_op jit(solution)/shard_map/ppermute | solution.py:24
  262.2 17.1 %collective-permute-start.17 = (bf16[768,384]{1,0:T(8,128)(2,1)S(1)}, bf16[768,384]{1,0:T(8,128)(2,1)S(1)}, u32[]{:S(2)}, u32[]{:S(2)}) collective-permute-start(bf16[768,384]{1,0:T(8,128)(2,1)S(1)} %collective-permute-done.15), channel_id=1, source_target_pairs={{0,1},{1,2},{2,3},{3,4},{4,5},{5,6},{6,7},{7,8},{8,9},{9,10},{10,1... | collective-permute-start | bytes 1769480 | tf_op jit(solution)/shard_map/ppermute | solution.py:19
  262.2 17.1 %collective-permute-start.18 = (bf16[768,384]{1,0:T(8,128)(2,1)S(1)}, bf16[768,384]{1,0:T(8,128)(2,1)S(1)}, u32[]{:S(2)}, u32[]{:S(2)}) collective-permute-start(bf16[768,384]{1,0:T(8,128)(2,1)S(1)} %collective-permute-done.16), channel_id=1, source_target_pairs={{0,15},{1,0},{2,1},{3,2},{4,3},{5,4},{6,5},{7,6},{8,7},{9,8},{10,9... | collective-permute-start | bytes 1769480 | tf_op jit(solution)/shard_map/ppermute | solution.py:24
  279.4 16.3 %collective-permute-start.19 = (bf16[768,384]{1,0:T(8,128)(2,1)S(1)}, bf16[768,384]{1,0:T(8,128)(2,1)S(1)}, u32[]{:S(2)}, u32[]{:S(2)}) collective-permute-start(bf16[768,384]{1,0:T(8,128)(2,1)S(1)} %collective-permute-done.17), channel_id=1, source_target_pairs={{0,1},{1,2},{2,3},{3,4},{4,5},{5,6},{6,7},{7,8},{8,9},{9,10},{10,1... | collective-permute-start | bytes 1769480 | tf_op jit(solution)/shard_map/ppermute | solution.py:19
  279.4 16.3 %collective-permute-start.20 = (bf16[768,384]{1,0:T(8,128)(2,1)S(1)}, bf16[768,384]{1,0:T(8,128)(2,1)S(1)}, u32[]{:S(2)}, u32[]{:S(2)}) collective-permute-start(bf16[768,384]{1,0:T(8,128)(2,1)S(1)} %collective-permute-done.18), channel_id=1, source_target_pairs={{0,15},{1,0},{2,1},{3,2},{4,3},{5,4},{6,5},{7,6},{8,7},{9,8},{10,9... | collective-permute-start | bytes 1769480 | tf_op jit(solution)/shard_map/ppermute | solution.py:24
  295.6 15.4 %collective-permute-start.21 = (bf16[768,384]{1,0:T(8,128)(2,1)S(1)}, bf16[768,384]{1,0:T(8,128)(2,1)S(1)}, u32[]{:S(2)}, u32[]{:S(2)}) collective-permute-start(bf16[768,384]{1,0:T(8,128)(2,1)S(1)} %collective-permute-done.19), channel_id=1, source_target_pairs={{0,1},{1,2},{2,3},{3,4},{4,5},{5,6},{6,7},{7,8},{8,9},{9,10},{10,1... | collective-permute-start | bytes 1769480 | tf_op jit(solution)/shard_map/ppermute | solution.py:19
  295.7 15.4 %collective-permute-start.22 = (bf16[768,384]{1,0:T(8,128)(2,1)S(1)}, bf16[768,384]{1,0:T(8,128)(2,1)}, u32[]{:S(2)}, u32[]{:S(2)}) collective-permute-start(bf16[768,384]{1,0:T(8,128)(2,1)S(1)} %collective-permute-done.20), channel_id=1, source_target_pairs={{0,15},{1,0},{2,1},{3,2},{4,3},{5,4},{6,5},{7,6},{8,7},{9,8},{10,9... | collective-permute-start | bytes 1769480 | tf_op jit(solution)/shard_map/ppermute | solution.py:24
  311.1 19.7 %collective-permute-start.24 = (bf16[768,384]{1,0:T(8,128)(2,1)}, bf16[768,384]{1,0:T(8,128)(2,1)S(1)}, u32[]{:S(2)}, u32[]{:S(2)}) collective-permute-start(bf16[768,384]{1,0:T(8,128)(2,1)} %collective-permute-done.22), channel_id=1, source_target_pairs={{0,15},{1,0},{2,1},{3,2},{4,3},{5,4},{6,5},{7,6},{8,7},{9,8},{10,9... | collective-permute-start | bytes 1769480 | tf_op jit(solution)/shard_map/ppermute | solution.py:24
  330.9 14.9 %collective-permute-start.26 = (bf16[768,384]{1,0:T(8,128)(2,1)S(1)}, bf16[768,384]{1,0:T(8,128)(2,1)S(1)}, u32[]{:S(2)}, u32[]{:S(2)}) collective-permute-start(bf16[768,384]{1,0:T(8,128)(2,1)S(1)} %collective-permute-done.24), channel_id=1, source_target_pairs={{0,15},{1,0},{2,1},{3,2},{4,3},{5,4},{6,5},{7,6},{8,7},{9,8},{10,9... | collective-permute-start | bytes 1769480 | tf_op jit(solution)/shard_map/ppermute | solution.py:24
  (24 other events, 592.7 us)
Sparse Core Ops, SparseCore 0:
  15.6 37.7 all-gather.4
  149.0 37.4 all-gather.6
  200.1 34.1 all-gather.8
  244.2 34.2 all-gather.10
